TPU v7x, 512 devices: a whole 4x4x16 slice. The times are simulated.
512 devices in a mesh: rowpt: 32 (over y, z_hi, core), colpt: 16 (over z_lo, x).
Axes of the slice: x: 4, y: 4, z: 16 (z_hi: 4, z_lo: 4; z = z_hi * 4 + z_lo), core: 2. Of those that a mesh axis runs over, the one named last changes fastest.
Arguments:
- x_pairs: float32 [4, 1024, 1024], P(None, 'rowpt', 'colpt'), may hold values from -6 to 6
- eps_val: float32 [1024], P('rowpt'), may hold values from -2 to -0.5
- eps_con: float32 [1024], P('colpt'), may hold values from 0.5 to 2
- orb_val: float32 [8192, 1024], P(('rowpt', 'colpt')), may hold values from -0.35 to 0.35
- orb_con: float32 [8192, 1024], P(('rowpt', 'colpt')), may hold values from -0.35 to 0.35
- screened_w: float32 [8192, 8192], P('rowpt', 'colpt'), may hold values from -0.0625 to 0.0625
Outputs:
- hx: float32 [4, 1024, 1024], P(None, 'rowpt', 'colpt')
All inputs are finite; a program needn't handle non-finite values.
Results may differ from a plain program's by a relative error of at most 0.00005.
Values sent between devices are 32-bit elements; how exact they have to be, the bound alone decides.
A program may use at most 64 MiB of HBM per device.

v0:
```python
import jax
import jax.numpy as jnp
from jax import lax
from jax.sharding import PartitionSpec as P

NP = 8192


def joined_along(pieces, dim):
    lengths = list(pieces.shape[1:])
    lengths[dim] *= pieces.shape[0]
    return jnp.moveaxis(pieces, 0, dim).reshape(lengths)


def copy_for_each(array, axis):
    copies = jnp.broadcast_to(array, (lax.axis_size(axis), *array.shape))
    return lax.all_to_all(copies, axis, split_axis=0, concat_axis=0, tiled=True)


def gathered_copies(array, axis, dim):
    return joined_along(copy_for_each(array, axis), dim)


def in_blocks(array, dim, devices):
    lengths = array.shape
    pieces = array.reshape(*lengths[:dim], devices, lengths[dim] // devices, *lengths[dim + 1 :])
    return jnp.moveaxis(pieces, dim, 0)


def sent_and_summed(array, axis, dim):
    devices = lax.axis_size(axis)
    pieces = lax.all_to_all(in_blocks(array, dim, devices), axis, 0, 0, tiled=True)
    return jnp.sum(pieces, axis=0)


def over_copies(array, axis):
    everything = copy_for_each(array, axis)
    return jnp.sum(everything, axis=0)


def reorder_points(values, outer, inner):
    width = values.shape[1]
    shaped = values.reshape(outer, inner, -1, width)
    return jnp.transpose(shaped, (1, 0, 2, 3)).reshape(-1, width)


def per_device(x_pairs, eps_val, eps_con, orb_val, orb_con, screened_w):
    nrow = lax.axis_size("rowpt")
    ncol = lax.axis_size("colpt")
    val_part = lax.all_to_all(orb_val, "rowpt", split_axis=1, concat_axis=0, tiled=True)
    val_mixed = gathered_copies(val_part, "colpt", 0)
    val_cols = reorder_points(val_mixed, ncol, nrow)
    con_part = lax.all_to_all(orb_con, "colpt", split_axis=1, concat_axis=0, tiled=True)
    con_cols = lax.all_gather(con_part, "rowpt", axis=0, tiled=True)
    block_pts = min(NP, 2048)
    nblocks = NP // block_pts
    vecs = x_pairs.shape[0]
    val_blocks = val_cols.reshape(nblocks, block_pts, val_cols.shape[1])
    con_blocks = con_cols.reshape(nblocks, block_pts, con_cols.shape[1])

    def density_block(pieces):
        val_piece, con_piece = pieces
        through = jnp.einsum("pc,bvc->bpv", con_piece, x_pairs, precision=lax.Precision.HIGHEST)
        return jnp.sum(through * val_piece[None], axis=2)

    partial_density = lax.map(density_block, (val_blocks, con_blocks))
    partial_density = jnp.transpose(partial_density, (1, 0, 2)).reshape(vecs, NP)
    column_share = sent_and_summed(partial_density, "colpt", 1)
    density = over_copies(column_share, "rowpt")
    screened_part = jnp.einsum("bq,pq->bp", density, screened_w, precision=lax.Precision.HIGHEST)
    row_total = over_copies(screened_part, "colpt")
    screened = gathered_copies(row_total, "rowpt", 1)
    pot_blocks = jnp.transpose(screened.reshape(vecs, nblocks, block_pts), (1, 0, 2))

    def kernel_block(total, pieces):
        val_piece, con_piece, pot_piece = pieces
        weighted = val_piece[None] * pot_piece[:, :, None]
        step = jnp.einsum("bpv,pc->bvc", weighted, con_piece, precision=lax.Precision.HIGHEST)
        return (total + step, None)

    start = jnp.zeros(x_pairs.shape, jnp.float32)
    kernel, unused = lax.scan(kernel_block, start, (val_blocks, con_blocks, pot_blocks))
    diff = eps_con[None, None, :] - eps_val[None, :, None]
    return diff * x_pairs + kernel


def solution(mesh):
    in_specs = (
        P(None, "rowpt", "colpt"),
        P("rowpt"),
        P("colpt"),
        P(("rowpt", "colpt"), None),
        P(("rowpt", "colpt"), None),
        P("rowpt", "colpt"),
    )
    out_specs = P(None, "rowpt", "colpt")
    return jax.shard_map(
        per_device, mesh=mesh, in_specs=in_specs, out_specs=out_specs, check_vma=False
    )
```

profile of v0, /device:TPU:33, one launch (start us, length us, event | category | flops | bytes accessed | tf_op | source)
XLA Modules:
  0.0 252.5 jit_solution(8417644518098035840)
XLA Ops:
  6.5 1.0 all_to_all.48
  8.3 7.9 %all-to-all-start.2 = ((f32[16,1,1024]{2,1,0:T(1,128)}), f32[16,1,1024]{2,1,0:T(1,128)S(1)}, u32[]{:S(2)}, u32[]{:S(2)}) async-start(f32[16,1,1024]{2,1,0:T(1,128)} %reshape.48), calls=%async_computation.2 | async-start | bytes 131072 | tf_op jit(solution)/shard_map/all_to_all | solution.py:53
  18.2 3.8 %all-to-all-done.2 = f32[16,1,1024]{2,1,0:T(1,128)S(1)} async-done(((f32[16,1,1024]{2,1,0:T(1,128)}), f32[16,1,1024]{2,1,0:T(1,128)S(1)}, u32[]{:S(2)}, u32[]{:S(2)}) %all-to-all-start.2) | async-done | bytes 65568 | tf_op jit(solution)/shard_map/all_to_all | solution.py:53
  22.0 17.3 %all-to-all-start = ((f32[32,1,512]{2,1,0:T(1,128)}), f32[32,1,512]{2,1,0:T(1,128)S(1)}, u32[]{:S(2)}, u32[]{:S(2)}) async-start(f32[32,1,512]{2,1,0:T(1,128)} %reshape.46), calls=%async_computation | async-start | bytes 131072 | tf_op jit(solution)/shard_map/all_to_all | solution.py:50
  41.4 14.1 %all-to-all-done = f32[32,1,512]{2,1,0:T(1,128)S(1)} async-done(((f32[32,1,512]{2,1,0:T(1,128)}), f32[32,1,512]{2,1,0:T(1,128)S(1)}, u32[]{:S(2)}, u32[]{:S(2)}) %all-to-all-start) | async-done | bytes 65568 | tf_op jit(solution)/shard_map/all_to_all | solution.py:50
  56.6 1.1 broadcast_in_dim.28
  57.7 3.6 %all-to-all-start.1 = ((f32[16,512,32]{1,2,0:T(8,128)}), f32[16,512,32]{1,2,0:T(8,128)S(1)}, u32[]{:S(2)}, u32[]{:S(2)}) async-start(f32[16,512,32]{1,2,0:T(8,128)} %broadcast_in_dim.28), calls=%async_computation.1 | async-start | bytes 2097152 | tf_op jit(solution)/shard_map/all_to_all | solution.py:17
  61.3 33.9 %all-to-all-done.1 = f32[16,512,32]{1,2,0:T(8,128)S(1)} async-done(((f32[16,512,32]{1,2,0:T(8,128)}), f32[16,512,32]{1,2,0:T(8,128)S(1)}, u32[]{:S(2)}, u32[]{:S(2)}) %all-to-all-start.1) | async-done | bytes 1048608 | tf_op jit(solution)/shard_map/all_to_all | solution.py:17
  95.1 2.7 %copy.50 = f32[16,512,32]{2,1,0:T(8,128)} copy(f32[16,512,32]{1,2,0:T(8,128)S(1)} %all-to-all-done.1) | data formatting | bytes 2097152 | tf_op jit(solution)/shard_map/all_to_all | solution.py:17
  97.8 4.7 %copy.51 = f32[32,16,16,32]{3,2,1,0:T(8,128)} copy(f32[32,16,16,32]{3,2,0,1:T(8,128)} %bitcast.61) | data formatting | bytes 2097152 | tf_op jit(solution)/shard_map/transpose | solution.py:44
  102.5 3.7 %copy.60 = f32[4,2048,32]{1,2,0:T(8,128)} copy(f32[4,2048,32]{2,1,0:T(8,128)} %bitcast.62) | data formatting | bytes 2097152
  106.2 37.6 %all-gather.2.cloned.1.call-done = f32[8192,64]{1,0:T(8,128)} async-done(((f32[256,64]{1,0:T(8,128)}), f32[8192,64]{1,0:T(8,128)}) %all-gather.2.cloned.1.call-update) | async-done | bytes 2097168 | tf_op jit(solution)/shard_map/all_gather | solution.py:54
  143.8 2.9 %copy.54 = f32[4,2048,64]{1,2,0:T(8,128)S(1)} copy(f32[4,2048,64]{2,1,0:T(8,128)} %bitcast.63) | data formatting | bytes 4194304 | tf_op jit(solution)/shard_map/while | solution.py:66
  146.6 8.2 %while.21 = (s32[]{:T(128)}, f32[4,4,2048]{2,1,0:T(4,128)S(1)}, f32[4,2048,64]{1,2,0:T(8,128)S(1)}, f32[4,32,64]{2,1,0:T(8,128)S(1)}, f32[4,2048,32]{1,2,0:T(8,128)}, /*index=5*/s32[]{:T(128)}) while((s32[]{:T(128)}, f32[4,4,2048]{2,1,0:T(4,128)S(1)}, f32[4,2048,64]{1,2,0:T(8,128)S(1)}, f32[4,32,64]{2,1,0:T(8,128)S(1)}, ...), condition=%wide.region_2.3_spmd, body=%wide.region_0.2_spmd.sunk | while | flops 201842688 | bytes 1474641 | solution.py:66
  146.7 1.0 dynamic-slice_bitcast_fusion.6
  147.6 1.0 fusion.21
  148.7 1.0 dynamic-slice_bitcast_fusion.6
  149.7 1.0 fusion.21
  150.8 1.0 dynamic-slice_bitcast_fusion.6
  151.7 1.0 fusion.21
  152.8 1.0 dynamic-slice_bitcast_fusion.6
  153.8 1.0 fusion.21
  155.2 14.8 %all_to_all.63 = f32[16,4,512]{2,1,0:T(4,128)S(1)} all-to-all(f32[16,4,512]{2,1,0:T(4,128)S(1)} %copy.57), channel_id=1, replica_groups=mesh['rowpt'=32,'colpt'=16] {'colpt'}, dimensions={0} | all-to-all | bytes 262144 | tf_op jit(solution)/shard_map/all_to_all | solution.py:32
  170.0 32.2 %all_to_all.64 = f32[32,4,512]{2,1,0:T(4,128)S(1)} all-to-all(f32[32,4,512]{2,1,0:T(4,128)S(1)} %broadcast_in_dim.30), channel_id=1, replica_groups=mesh['rowpt'=32,'colpt'=16] {'rowpt'}, dimensions={0} | all-to-all | bytes 524288 | tf_op jit(solution)/shard_map/all_to_all | solution.py:17
  202.8 9.1 %all_to_all.65 = f32[16,4,256]{2,1,0:T(4,128)S(1)} all-to-all(f32[16,4,256]{2,1,0:T(4,128)S(1)} %broadcast_in_dim.31), channel_id=1, replica_groups=mesh['rowpt'=32,'colpt'=16] {'colpt'}, dimensions={0} | all-to-all | bytes 131072 | tf_op jit(solution)/shard_map/all_to_all | solution.py:17
  212.6 5.3 %all-to-all-start.6 = ((f32[32,4,256]{2,1,0:T(4,128)}), f32[32,4,256]{2,1,0:T(4,128)S(1)}, u32[]{:S(2)}, u32[]{:S(2)}) async-start(f32[32,4,256]{2,1,0:T(4,128)} %broadcast_in_dim.32), calls=%async_computation.6 | async-start | bytes 262144 | tf_op jit(solution)/shard_map/all_to_all | solution.py:17
  218.0 19.0 %all-to-all-done.6 = f32[32,4,256]{2,1,0:T(4,128)S(1)} async-done(((f32[32,4,256]{2,1,0:T(4,128)}), f32[32,4,256]{2,1,0:T(4,128)S(1)}, u32[]{:S(2)}, u32[]{:S(2)}) %all-to-all-start.6) | async-done | bytes 131104 | tf_op jit(solution)/shard_map/all_to_all | solution.py:17
  236.9 8.0 %while.22 = (s32[]{:T(128)}, f32[4,32,64]{2,1,0:T(8,128)S(1)}, f32[4,2048,32]{1,2,0:T(8,128)}, f32[4,4,2048]{2,1,0:T(4,128)S(1)}, f32[4,2048,64]{1,2,0:T(8,128)S(1)}, /*index=5*/s32[]{:T(128)}, s32[]{:T(128)}) while((s32[]{:T(128)}, f32[4,32,64]{2,1,0:T(8,128)S(1)}, f32[4,2048,32]{1,2,0:T(8,128)}, f32[4,4,2048]{2,1,0:T(4,128)S(1)}, ...), condition=%wide.region_7.8_spmd.clone, body=%wide.region_6.7_spmd.clone.sunk | while | flops 201605120 | bytes 1507427 | solution.py:82
  237.9 1.0 convolution_add_fusion.2
  239.9 1.0 convolution_add_fusion.2
  241.9 1.0 convolution_add_fusion.2
  244.0 1.0 convolution_add_fusion.2
  (47 shorter events, 12.2 us)
Async XLA Ops:
  6.5 195.7 %copy-start = (f32[256,512]{1,0:T(8,128)S(1)}, f32[256,512]{1,0:T(8,128)}, u32[]{:S(2)}) copy-start(f32[256,512]{1,0:T(8,128)} %param.15) | copy-start | bytes 1572868
  8.3 13.7 %all-to-all-start.2 = ((f32[16,1,1024]{2,1,0:T(1,128)}), f32[16,1,1024]{2,1,0:T(1,128)S(1)}, u32[]{:S(2)}, u32[]{:S(2)}) async-start(f32[16,1,1024]{2,1,0:T(1,128)} %reshape.48), calls=%async_computation.2 | async-start | bytes 131072 | tf_op jit(solution)/shard_map/all_to_all | solution.py:53
  22.0 33.5 %all-to-all-start = ((f32[32,1,512]{2,1,0:T(1,128)}), f32[32,1,512]{2,1,0:T(1,128)S(1)}, u32[]{:S(2)}, u32[]{:S(2)}) async-start(f32[32,1,512]{2,1,0:T(1,128)} %reshape.46), calls=%async_computation | async-start | bytes 131072 | tf_op jit(solution)/shard_map/all_to_all | solution.py:50
  39.3 104.5 %all-gather.2.cloned.1.call-start = ((), (), s32[]{:S(2)}) async-start(), calls=%async_computation.7 | async-start | bytes 4325376 | tf_op jit(solution)/shard_map/all_gather | solution.py:54
  57.7 37.4 %all-to-all-start.1 = ((f32[16,512,32]{1,2,0:T(8,128)}), f32[16,512,32]{1,2,0:T(8,128)S(1)}, u32[]{:S(2)}, u32[]{:S(2)}) async-start(f32[16,512,32]{1,2,0:T(8,128)} %broadcast_in_dim.28), calls=%async_computation.1 | async-start | bytes 2097152 | tf_op jit(solution)/shard_map/all_to_all | solution.py:17
  143.8 2.9 %copy-start.1 = (f32[4,32,64]{2,1,0:T(8,128)S(1)}, f32[4,32,64]{2,1,0:T(8,128)}, u32[]{:S(2)}) copy-start(f32[4,32,64]{2,1,0:T(8,128)} %param.10) | copy-start | bytes 98308
  154.9 63.0 %copy-start.2 = (f32[32]{0:T(128)S(1)}, f32[32]{0:T(128)}, u32[]{:S(2)}) copy-start(f32[32]{0:T(128)} %param.11) | copy-start | bytes 388
  154.9 63.0 %copy-start.3 = (f32[64]{0:T(128)S(1)}, f32[64]{0:T(128)}, u32[]{:S(2)}) copy-start(f32[64]{0:T(128)} %param.12) | copy-start | bytes 772
  212.6 24.3 %all-to-all-start.6 = ((f32[32,4,256]{2,1,0:T(4,128)}), f32[32,4,256]{2,1,0:T(4,128)S(1)}, u32[]{:S(2)}, u32[]{:S(2)}) async-start(f32[32,4,256]{2,1,0:T(4,128)} %broadcast_in_dim.32), calls=%async_computation.6 | async-start | bytes 262144 | tf_op jit(solution)/shard_map/all_to_all | solution.py:17
Sparse Core Ops, SparseCore 0:
  43.2 100.4 all-gather.1
where the time goes:
time: 253 us; the launch traced here: 252 us
  waiting for transfers between devices  108 us (43%)
  blocking collectives  56 us (22%)
  starting transfers between devices  34.1 us (13%)
  local copies, waits for them, and re-layouts  29 us (11%)
  between operations  13.6 us (5%)
  matrix products  8.63 us (3%)
    all_to_all x2, waiting for transfers between devices, copy_for_each(): return lax.all_to_all(copies, axis, split_axis=0, concat_axis=0, tiled=True)  52.8 us
    all_to_all x2, blocking collectives, copy_for_each(): return lax.all_to_all(copies, axis, split_axis=0, concat_axis=0, tiled=True)  41.3 us
    all_gather x1, waiting for transfers between devices, per_device(): con_cols = lax.all_gather(con_part, 'rowpt', axis=0, tiled=True)  37.6 us
    all_to_all x1, starting transfers between devices, per_device(): lax.all_to_all(orb_val, 'rowpt', split_axis=1, concat_axis=0, tiled=True)  17.3 us
    all_to_all x1, blocking collectives, sent_and_summed(): lax.all_to_all(in_blocks(array, dim, devices), axis, 0, 0, tiled=True)  14.8 us
    all_to_all x1, waiting for transfers between devices, per_device(): lax.all_to_all(orb_val, 'rowpt', split_axis=1, concat_axis=0, tiled=True)  14.1 us
    all_to_all x2, starting transfers between devices, copy_for_each(): return lax.all_to_all(copies, axis, split_axis=0, concat_axis=0, tiled=True)  8.85 us
    all_to_all x1, starting transfers between devices, per_device(): lax.all_to_all(orb_con, 'colpt', split_axis=1, concat_axis=0, tiled=True)  7.92 us
  transfers between devices with their start and end apart: 5, of which 5 were waited for; matrix products, arithmetic and copies ran while one was open for 6% of the time, Pallas kernels for 0%

commit v1 on v0

--- a/solution.py
+++ b/solution.py
@@ -1,9 +1,21 @@
+import functools
 import jax
 import jax.numpy as jnp
 from jax import lax
 from jax.sharding import PartitionSpec as P
 
 NP = 8192
+
+
+def guide_ways(x_local, dim_at):
+    y = lax.axis_size("rowpt")
+    z = jnp.stack([x_local] * y)
+    r2 = lax.all_to_all(z, "rowpt", 0, 0)
+    block_next = jnp.concatenate(r2, axis=dim_at)
+    return block_next
+
+
+lay_wires = functools.partial(guide_ways, dim_at=0)
 
 
 def joined_along(pieces, dim):
@@ -51,7 +63,7 @@
     val_mixed = gathered_copies(val_part, "colpt", 0)
     val_cols = reorder_points(val_mixed, ncol, nrow)
     con_part = lax.all_to_all(orb_con, "colpt", split_axis=1, concat_axis=0, tiled=True)
-    con_cols = lax.all_gather(con_part, "rowpt", axis=0, tiled=True)
+    con_cols = lay_wires(con_part)
     block_pts = min(NP, 2048)
     nblocks = NP // block_pts
     vecs = x_pairs.shape[0]

time: 253 us -> 289 us (1.14)
  waiting for transfers between devices: 108 us -> 149 us
  between operations: 13.6 us -> 0.2 us
  local copies, waits for them, and re-layouts: 29 us -> 36.9 us
  starting transfers between devices: 34.1 us -> 39.9 us
  blocking collectives: 56 us -> 51 us
    all_to_all x0 -> x1, waiting for transfers between devices: none -> 88.1 us  [guide_ways(): r2 = lax.all_to_all(z, 'rowpt', 0, 0)]
    all_gather x1 -> x0, waiting for transfers between devices: 37.6 us -> none  [per_device(): con_cols = lax.all_gather(con_part, 'rowpt', axis=0, tiled=True)]
    all_to_all x2, waiting for transfers between devices: 52.8 us -> 42.5 us  [copy_for_each(): return lax.all_to_all(copies, axis, split_axis=0, concat_axis=0, tiled=True)]
    all_to_all x0 -> x1, starting transfers between devices: none -> 6.08 us  [guide_ways(): r2 = lax.all_to_all(z, 'rowpt', 0, 0)]
    another operation x0 -> x3, local copies, waits for them, and re-layouts: none -> 5.03 us  [the longest x1 3.16 us: per_device(): con_blocks = con_cols.reshape(nblocks, block_pts, con_cols.shape[1])]
    all_to_all x1, blocking collectives: 14.8 us -> 10.5 us  [sent_and_summed(): lax.all_to_all(in_blocks(array, dim, devices), axis, 0, 0, tiled=True)]
    unnamed x13 -> x15, local copies, waits for them, and re-layouts: 6.1 us -> 5.37 us
  transfers between devices with their start and end apart: 5 -> 5, of which waited for: 5 -> 5; matrix products, arithmetic and copies ran while one was open for 6% -> 5% of each run, Pallas kernels for 0% -> 0%
where the time goes in v1:
time: 289 us; the launch traced here: 288 us
  waiting for transfers between devices  149 us (52%)
  blocking collectives  51 us (18%)
  starting transfers between devices  39.9 us (14%)
  local copies, waits for them, and re-layouts  36.9 us (13%)
  matrix products  8.63 us (3%)
    all_to_all x1, waiting for transfers between devices, guide_ways(): r2 = lax.all_to_all(z, 'rowpt', 0, 0)  88.1 us
    all_to_all x2, waiting for transfers between devices, copy_for_each(): return lax.all_to_all(copies, axis, split_axis=0, concat_axis=0, tiled=True)  42.5 us
    all_to_all x2, blocking collectives, copy_for_each(): return lax.all_to_all(copies, axis, split_axis=0, concat_axis=0, tiled=True)  40.5 us
    all_to_all x1, starting transfers between devices, per_device(): lax.all_to_all(orb_val, 'rowpt', split_axis=1, concat_axis=0, tiled=True)  17.7 us
    all_to_all x1, waiting for transfers between devices, per_device(): lax.all_to_all(orb_val, 'rowpt', split_axis=1, concat_axis=0, tiled=True)  14.3 us
    all_to_all x2, starting transfers between devices, copy_for_each(): return lax.all_to_all(copies, axis, split_axis=0, concat_axis=0, tiled=True)  10.5 us
    all_to_all x1, blocking collectives, sent_and_summed(): lax.all_to_all(in_blocks(array, dim, devices), axis, 0, 0, tiled=True)  10.5 us
    all_to_all x1, starting transfers between devices, guide_ways(): r2 = lax.all_to_all(z, 'rowpt', 0, 0)  6.08 us
  transfers between devices with their start and end apart: 5, of which 5 were waited for; matrix products, arithmetic and copies ran while one was open for 5% of the time, Pallas kernels for 0%

profile of v1, /device:TPU:33, one launch (start us, length us, event | category | flops | bytes accessed | tf_op | source)
XLA Modules:
  0.0 288.4 jit_solution(17308413831673159120)
XLA Ops:
  0.0 1.0 all_to_all.44
  2.0 17.7 %all-to-all-start = ((f32[32,1,512]{2,1,0:T(1,128)}), f32[32,1,512]{2,1,0:T(1,128)S(1)}, u32[]{:S(2)}, u32[]{:S(2)}) async-start(f32[32,1,512]{2,1,0:T(1,128)} %reshape.45), calls=%async_computation | async-start | bytes 131072 | tf_op jit(solution)/shard_map/all_to_all | solution.py:62
  21.4 14.3 %all-to-all-done = f32[32,1,512]{2,1,0:T(1,128)S(1)} async-done(((f32[32,1,512]{2,1,0:T(1,128)}), f32[32,1,512]{2,1,0:T(1,128)S(1)}, u32[]{:S(2)}, u32[]{:S(2)}) %all-to-all-start) | async-done | bytes 65568 | tf_op jit(solution)/shard_map/all_to_all | solution.py:62
  35.7 5.6 %all-to-all-start.2 = ((f32[16,1,1024]{2,1,0:T(1,128)}), f32[16,1,1024]{2,1,0:T(1,128)S(1)}, u32[]{:S(2)}, u32[]{:S(2)}) async-start(f32[16,1,1024]{2,1,0:T(1,128)} %reshape.47), calls=%async_computation.2 | async-start | bytes 131072 | tf_op jit(solution)/shard_map/all_to_all | solution.py:65
  43.0 4.1 %all-to-all-done.2 = f32[16,1,1024]{2,1,0:T(1,128)S(1)} async-done(((f32[16,1,1024]{2,1,0:T(1,128)}), f32[16,1,1024]{2,1,0:T(1,128)S(1)}, u32[]{:S(2)}, u32[]{:S(2)}) %all-to-all-start.2) | async-done | bytes 65568 | tf_op jit(solution)/shard_map/all_to_all | solution.py:65
  47.1 1.1 broadcast_in_dim.28
  48.2 5.2 %all-to-all-start.1 = ((f32[16,512,32]{1,2,0:T(8,128)}), f32[16,512,32]{1,2,0:T(8,128)S(1)}, u32[]{:S(2)}, u32[]{:S(2)}) async-start(f32[16,512,32]{1,2,0:T(8,128)} %broadcast_in_dim.28), calls=%async_computation.1 | async-start | bytes 2097152 | tf_op jit(solution)/shard_map/all_to_all | solution.py:29
  54.4 23.6 %all-to-all-done.1 = f32[16,512,32]{1,2,0:T(8,128)S(1)} async-done(((f32[16,512,32]{1,2,0:T(8,128)}), f32[16,512,32]{1,2,0:T(8,128)S(1)}, u32[]{:S(2)}, u32[]{:S(2)}) %all-to-all-start.1) | async-done | bytes 1048608 | tf_op jit(solution)/shard_map/all_to_all | solution.py:29
  78.0 1.8 stack.5
  79.8 6.1 %all-to-all-start.3 = ((f32[32,256,64]{1,2,0:T(8,128)}), f32[32,256,64]{1,2,0:T(8,128)S(1)}, u32[]{:S(2)}, u32[]{:S(2)}) async-start(f32[32,256,64]{1,2,0:T(8,128)} %stack.5), calls=%async_computation.3 | async-start | bytes 4194304 | tf_op jit(solution)/shard_map/all_to_all | solution.py:13
  85.9 3.6 %copy.52 = f32[16,512,32]{2,1,0:T(8,128)} copy(f32[16,512,32]{1,2,0:T(8,128)} %copy-done.1) | data formatting | bytes 2097152 | tf_op jit(solution)/shard_map/all_to_all | solution.py:29
  89.5 4.7 %copy.53 = f32[32,16,16,32]{3,2,1,0:T(8,128)} copy(f32[32,16,16,32]{3,2,0,1:T(8,128)} %bitcast.62) | data formatting | bytes 2097152 | tf_op jit(solution)/shard_map/transpose | solution.py:56
  94.2 3.6 %copy.63 = f32[4,2048,32]{1,2,0:T(8,128)} copy(f32[4,2048,32]{2,1,0:T(8,128)} %bitcast.63) | data formatting | bytes 2097152
  97.8 88.1 %all-to-all-done.3 = f32[32,256,64]{1,2,0:T(8,128)S(1)} async-done(((f32[32,256,64]{1,2,0:T(8,128)}), f32[32,256,64]{1,2,0:T(8,128)S(1)}, u32[]{:S(2)}, u32[]{:S(2)}) %all-to-all-start.3) | async-done | bytes 2097184 | tf_op jit(solution)/shard_map/all_to_all | solution.py:13
  185.9 2.6 copy.56
  188.5 3.2 %reshape_reshape.17 = f32[4,2048,64]{1,0,2:T(4,128)} reshape(f32[32,256,64]{1,0,2:T(8,128)} %copy.56) | data formatting | bytes 4194304 | tf_op jit(solution)/shard_map/reshape;reshape | solution.py:71
  191.7 2.8 copy.57
  194.5 8.2 %while.21 = (s32[]{:T(128)}, f32[4,4,2048]{2,1,0:T(4,128)S(1)}, f32[4,2048,64]{1,2,0:T(8,128)S(1)}, f32[4,32,64]{2,1,0:T(8,128)S(1)}, f32[4,2048,32]{1,2,0:T(8,128)}, /*index=5*/s32[]{:T(128)}) while((s32[]{:T(128)}, f32[4,4,2048]{2,1,0:T(4,128)S(1)}, f32[4,2048,64]{1,2,0:T(8,128)S(1)}, f32[4,32,64]{2,1,0:T(8,128)S(1)}, ...), condition=%wide.region_2.3_spmd, body=%wide.region_0.2_spmd.sunk | while | flops 201842688 | bytes 1474641 | solution.py:78
  195.5 1.0 fusion.21
  197.5 1.0 fusion.21
  199.6 1.0 fusion.21
  201.7 1.0 fusion.21
  203.0 10.5 %all_to_all.65 = f32[16,4,512]{2,1,0:T(4,128)S(1)} all-to-all(f32[16,4,512]{2,1,0:T(4,128)S(1)} %copy.60), channel_id=1, replica_groups=mesh['rowpt'=32,'colpt'=16] {'colpt'}, dimensions={0} | all-to-all | bytes 262144 | tf_op jit(solution)/shard_map/all_to_all | solution.py:44
  213.6 31.1 %all_to_all.66 = f32[32,4,512]{2,1,0:T(4,128)S(1)} all-to-all(f32[32,4,512]{2,1,0:T(4,128)S(1)} %broadcast_in_dim.30), channel_id=1, replica_groups=mesh['rowpt'=32,'colpt'=16] {'rowpt'}, dimensions={0} | all-to-all | bytes 524288 | tf_op jit(solution)/shard_map/all_to_all | solution.py:29
  245.3 9.4 %all_to_all.67 = f32[16,4,256]{2,1,0:T(4,128)S(1)} all-to-all(f32[16,4,256]{2,1,0:T(4,128)S(1)} %broadcast_in_dim.31), channel_id=1, replica_groups=mesh['rowpt'=32,'colpt'=16] {'colpt'}, dimensions={0} | all-to-all | bytes 131072 | tf_op jit(solution)/shard_map/all_to_all | solution.py:29
  255.4 5.3 %all-to-all-start.7 = ((f32[32,4,256]{2,1,0:T(4,128)}), f32[32,4,256]{2,1,0:T(4,128)S(1)}, u32[]{:S(2)}, u32[]{:S(2)}) async-start(f32[32,4,256]{2,1,0:T(4,128)} %broadcast_in_dim.32), calls=%async_computation.7 | async-start | bytes 262144 | tf_op jit(solution)/shard_map/all_to_all | solution.py:29
  260.8 19.0 %all-to-all-done.7 = f32[32,4,256]{2,1,0:T(4,128)S(1)} async-done(((f32[32,4,256]{2,1,0:T(4,128)}), f32[32,4,256]{2,1,0:T(4,128)S(1)}, u32[]{:S(2)}, u32[]{:S(2)}) %all-to-all-start.7) | async-done | bytes 131104 | tf_op jit(solution)/shard_map/all_to_all | solution.py:29
  279.7 8.0 %while.22 = (s32[]{:T(128)}, f32[4,32,64]{2,1,0:T(8,128)S(1)}, f32[4,2048,32]{1,2,0:T(8,128)}, f32[4,4,2048]{2,1,0:T(4,128)S(1)}, f32[4,2048,64]{1,2,0:T(8,128)S(1)}, /*index=5*/s32[]{:T(128)}, s32[]{:T(128)}) while((s32[]{:T(128)}, f32[4,32,64]{2,1,0:T(8,128)S(1)}, f32[4,2048,32]{1,2,0:T(8,128)}, f32[4,4,2048]{2,1,0:T(4,128)S(1)}, ...), condition=%wide.region_7.8_spmd.clone, body=%wide.region_6.7_spmd.clone.sunk | while | flops 201605120 | bytes 1507427 | solution.py:94
  280.7 1.0 convolution_add_fusion.2
  282.7 1.0 convolution_add_fusion.2
  284.8 1.0 convolution_add_fusion.2
  286.8 1.0 convolution_add_fusion.2
  (52 shorter events, 15.5 us)
Async XLA Ops:
  0.0 244.8 %copy-start = (f32[256,512]{1,0:T(8,128)S(1)}, f32[256,512]{1,0:T(8,128)}, u32[]{:S(2)}) copy-start(f32[256,512]{1,0:T(8,128)} %param.15) | copy-start | bytes 1572868
  2.0 33.7 %all-to-all-start = ((f32[32,1,512]{2,1,0:T(1,128)}), f32[32,1,512]{2,1,0:T(1,128)S(1)}, u32[]{:S(2)}, u32[]{:S(2)}) async-start(f32[32,1,512]{2,1,0:T(1,128)} %reshape.45), calls=%async_computation | async-start | bytes 131072 | tf_op jit(solution)/shard_map/all_to_all | solution.py:62
  35.7 11.4 %all-to-all-start.2 = ((f32[16,1,1024]{2,1,0:T(1,128)}), f32[16,1,1024]{2,1,0:T(1,128)S(1)}, u32[]{:S(2)}, u32[]{:S(2)}) async-start(f32[16,1,1024]{2,1,0:T(1,128)} %reshape.47), calls=%async_computation.2 | async-start | bytes 131072 | tf_op jit(solution)/shard_map/all_to_all | solution.py:65
  48.2 29.8 %all-to-all-start.1 = ((f32[16,512,32]{1,2,0:T(8,128)}), f32[16,512,32]{1,2,0:T(8,128)S(1)}, u32[]{:S(2)}, u32[]{:S(2)}) async-start(f32[16,512,32]{1,2,0:T(8,128)} %broadcast_in_dim.28), calls=%async_computation.1 | async-start | bytes 2097152 | tf_op jit(solution)/shard_map/all_to_all | solution.py:29
  78.0 1.8 copy-start.1
  79.8 106.1 %all-to-all-start.3 = ((f32[32,256,64]{1,2,0:T(8,128)}), f32[32,256,64]{1,2,0:T(8,128)S(1)}, u32[]{:S(2)}, u32[]{:S(2)}) async-start(f32[32,256,64]{1,2,0:T(8,128)} %stack.5), calls=%async_computation.3 | async-start | bytes 4194304 | tf_op jit(solution)/shard_map/all_to_all | solution.py:13
  191.7 2.8 copy-start.2
  202.7 58.0 %copy-start.3 = (f32[32]{0:T(128)S(1)}, f32[32]{0:T(128)}, u32[]{:S(2)}) copy-start(f32[32]{0:T(128)} %param.11) | copy-start | bytes 388
  202.7 58.0 %copy-start.4 = (f32[64]{0:T(128)S(1)}, f32[64]{0:T(128)}, u32[]{:S(2)}) copy-start(f32[64]{0:T(128)} %param.12) | copy-start | bytes 772
  255.4 24.3 %all-to-all-start.7 = ((f32[32,4,256]{2,1,0:T(4,128)}), f32[32,4,256]{2,1,0:T(4,128)S(1)}, u32[]{:S(2)}, u32[]{:S(2)}) async-start(f32[32,4,256]{2,1,0:T(4,128)} %broadcast_in_dim.32), calls=%async_computation.7 | async-start | bytes 262144 | tf_op jit(solution)/shard_map/all_to_all | solution.py:29
